TPU v7x, 256 devices: a whole 4x4x8 slice. The times are simulated.
256 devices in a mesh: gx: 8 (over y, x_lo), gy: 4 (over x_hi, core), gz: 8 (over z).
Axes of the slice: x: 4 (x_hi: 2, x_lo: 2; x = x_hi * 2 + x_lo), y: 4, z: 8, core: 2. Of those that a mesh axis runs over, the one named last changes fastest.
Arguments:
- tensor_blocks: bfloat16 [8, 4, 8, 3, 128, 128, 128], P('gx', 'gy', 'gz'), may hold values from 0 to 3
- fiber_mask: int32 [8, 4, 8, 3, 128, 128], P('gx', 'gy', 'gz'), may hold values 0 or 1
- block_coords: int32 [8, 4, 8, 3, 3], P('gx', 'gy', 'gz'), may hold values from 0 to 7, as said below
- block_counts: int32 [8, 4, 8], P('gx', 'gy', 'gz'), may hold values from 0 to 3, as said below
- factor_a: bfloat16 [8, 512, 256], P('gx', ('gy', 'gz')), may hold values from -0.59765625 to 0.59765625
- factor_b: bfloat16 [4, 1024, 256], P('gy', ('gx', 'gz')), may hold values from -0.59765625 to 0.59765625
- factor_c: bfloat16 [8, 512, 256], P('gz', ('gx', 'gy')), may hold values from -0.59765625 to 0.59765625
Outputs:
- grad_a: float32 [8, 512, 256], P('gx', ('gy', 'gz'))
- grad_b: float32 [4, 1024, 256], P('gy', ('gx', 'gz'))
- grad_c: float32 [8, 512, 256], P('gz', ('gx', 'gy'))
Inputs may be any that keep to these rules, and one draw needn't show every extreme that they name: `block_counts`: some sub-box holds exactly 3 blocks and some holds none, in every draw; slots at and past a sub-box's count hold no block. `block_coords`: the 3 columns of one sub-box name distinct blocks; row 0 is below 4, row 1 below 8, row 2 below 4.
All inputs are finite; a program needn't handle non-finite values. No bound on the sum of `fiber_mask` on one device may be relied on, other than what follows from the above.
Results may differ from a plain program's by a relative error of at most 0.0014.
Values may be sent and summed in bfloat16 or wider, within the bound.
A program may use at most 128 MiB of HBM per device.

v0:
```python
from functools import partial

import jax
import jax.numpy as jnp
from jax import lax
from jax.sharding import PartitionSpec as P

R = 256
BLK = 128
SLOTS = 3


def block_terms(rows_a, rows_b, rows_c, entries, fibers):
    khatri = (
        rows_b[:, None, :].astype(jnp.float32) * rows_c[None, :, :].astype(jnp.float32)
    ).astype(jnp.bfloat16)
    khatri = khatri.reshape(BLK * BLK, R)
    log_rate = jnp.einsum("ur,kr->uk", rows_a, khatri, preferred_element_type=jnp.float32)
    weight = fibers.astype(jnp.float32).reshape(BLK, BLK, 1)
    misfit = weight * (jnp.exp(log_rate.reshape(BLK, BLK, BLK)) - entries.astype(jnp.float32)) / BLK
    misfit = misfit.astype(jnp.bfloat16).reshape(BLK, BLK * BLK)
    part_a = jnp.dot(misfit, khatri, preferred_element_type=jnp.float32)
    folded = jnp.einsum("uk,ur->kr", misfit, rows_a, preferred_element_type=jnp.float32)
    folded = folded.astype(jnp.bfloat16).reshape(BLK, BLK, R)
    part_b = jnp.einsum("vwr,wr->vr", folded, rows_c, preferred_element_type=jnp.float32)
    part_c = jnp.einsum("vwr,vr->wr", folded, rows_b, preferred_element_type=jnp.float32)
    return (part_a, part_b, part_c)


def add_rows(total, start, part):
    current = lax.dynamic_slice_in_dim(total, start, BLK, 0)
    return lax.dynamic_update_slice_in_dim(total, current + part, start, 0)


def add_block(slot_index, coords, tensor_blocks, fiber_mask, slabs, totals):
    slab_rows_a, slab_rows_b, slab_rows_c = slabs
    grad_a, grad_b, grad_c = totals
    start_a = coords[0, slot_index] * BLK
    start_b = coords[1, slot_index] * BLK
    start_c = coords[2, slot_index] * BLK
    rows_a = lax.dynamic_slice_in_dim(slab_rows_a, start_a, BLK, 0)
    rows_b = lax.dynamic_slice_in_dim(slab_rows_b, start_b, BLK, 0)
    rows_c = lax.dynamic_slice_in_dim(slab_rows_c, start_c, BLK, 0)
    entries = tensor_blocks[0, 0, 0, slot_index]
    fibers = fiber_mask[0, 0, 0, slot_index]
    part_a, part_b, part_c = block_terms(rows_a, rows_b, rows_c, entries, fibers)
    return (
        add_rows(grad_a, start_a, part_a),
        add_rows(grad_b, start_b, part_b),
        add_rows(grad_c, start_c, part_c),
    )


def keep_totals(totals):
    return totals


def per_device(tensor_blocks, fiber_mask, block_coords, block_counts, factor_a, factor_b, factor_c):
    slab_rows_a = lax.all_gather(factor_a, ("gy", "gz"), axis=1, tiled=True)[0]
    slab_rows_b = lax.all_gather(factor_b, ("gx", "gz"), axis=1, tiled=True)[0]
    slab_rows_c = lax.all_gather(factor_c, ("gx", "gy"), axis=1, tiled=True)[0]
    slabs = (slab_rows_a, slab_rows_b, slab_rows_c)
    filled = block_counts[0, 0, 0]
    coords = block_coords[0, 0, 0]
    totals = (
        jnp.zeros(slab_rows_a.shape, jnp.float32),
        jnp.zeros(slab_rows_b.shape, jnp.float32),
        jnp.zeros(slab_rows_c.shape, jnp.float32),
    )
    for slot_index in range(SLOTS):
        adder = partial(add_block, slot_index, coords, tensor_blocks, fiber_mask, slabs)
        totals = lax.cond(slot_index < filled, adder, keep_totals, totals)
    terms_a, terms_b, terms_c = totals
    grad_a = lax.psum_scatter(terms_a[None], ("gy", "gz"), scatter_dimension=1, tiled=True)
    grad_b = lax.psum_scatter(terms_b[None], ("gx", "gz"), scatter_dimension=1, tiled=True)
    grad_c = lax.psum_scatter(terms_c[None], ("gx", "gy"), scatter_dimension=1, tiled=True)
    return (grad_a, grad_b, grad_c)


def solution(mesh):
    placed = (
        P("gx", "gy", "gz", None, None, None, None),
        P("gx", "gy", "gz", None, None, None),
        P("gx", "gy", "gz", None, None),
        P("gx", "gy", "gz"),
        P("gx", ("gy", "gz"), None),
        P("gy", ("gx", "gz"), None),
        P("gz", ("gx", "gy"), None),
    )
    return jax.shard_map(
        per_device,
        mesh=mesh,
        in_specs=placed,
        out_specs=(
            P("gx", ("gy", "gz"), None),
            P("gy", ("gx", "gz"), None),
            P("gz", ("gx", "gy"), None),
        ),
        check_vma=False,
    )
```

profile of v0, /device:TPU:4, one launch (start us, length us, event | category | flops | bytes accessed | tf_op | source)
XLA Modules:
  0.0 952.0 jit_solution(9491583259348897552)
XLA Ops:
  7.2 0.0 reduce-scatter.4.cloned.1.call-start
  7.2 161.8 %all_gather.10 = bf16[1,1024,256]{2,1,0:T(8,128)(2,1)S(1)} all-gather(bf16[1,16,256]{2,1,0:T(8,128)(2,1)} %param.18), channel_id=1, replica_groups=mesh['gx'=8,'gy'=4,'gz'=8] {'gx','gz'}, dimensions={1}, use_global_device_ids=true | all-gather | bytes 532480 | tf_op jit(solution)/shard_map/all_gather | solution.py:60
  169.0 65.1 %all_gather.9 = bf16[1,512,256]{2,1,0:T(8,128)(2,1)S(1)} all-gather(bf16[1,16,256]{2,1,0:T(8,128)(2,1)} %param.17), channel_id=1, replica_groups=mesh['gx'=8,'gy'=4,'gz'=8] {'gy','gz'}, dimensions={1}, use_global_device_ids=true | all-gather | bytes 270336 | tf_op jit(solution)/shard_map/all_gather | solution.py:59
  234.1 36.9 %all_gather.11 = bf16[1,512,256]{2,1,0:T(8,128)(2,1)S(1)} all-gather(bf16[1,16,256]{2,1,0:T(8,128)(2,1)} %param.19), channel_id=1, replica_groups=mesh['gx'=8,'gy'=4,'gz'=8] {'gx','gy'}, dimensions={1}, use_global_device_ids=true | all-gather | bytes 270336 | tf_op jit(solution)/shard_map/all_gather | solution.py:61
  271.0 0.7 copy.72
  272.4 2.7 conditional.3
  272.4 1.1 broadcast_in_dim.4
  273.5 0.8 broadcast.25
  274.3 0.8 broadcast.25.clone
  275.1 0.0 reduce-scatter.4.cloned.1.call-update
  275.1 0.0 reduce-scatter.8.cloned.1.call-start
  275.2 0.7 reduce-scatter.8.cloned.1.call-update
  275.9 0.0 reduce-scatter.6.cloned.1.call-start
  275.9 0.7 reduce-scatter.6.cloned.1.call-update
  276.6 211.2 %reduce-scatter.4.cloned.1.call-done = f32[1,16,256]{2,1,0:T(8,128)} async-done(((f32[1,512,256]{2,1,0:T(8,128)}), f32[1,16,256]{2,1,0:T(8,128)}) %reduce-scatter.4.cloned.1.call-update) | async-done | bytes 16400 | tf_op jit(solution)/shard_map/reduce_scatter | solution.py:74
  487.8 133.6 %reduce-scatter.8.cloned.1.call-done = f32[1,16,256]{2,1,0:T(8,128)} async-done(((f32[1,512,256]{2,1,0:T(8,128)}), f32[1,16,256]{2,1,0:T(8,128)}) %reduce-scatter.8.cloned.1.call-update) | async-done | bytes 16400 | tf_op jit(solution)/shard_map/reduce_scatter | solution.py:76
  621.4 324.0 %reduce-scatter.6.cloned.1.call-done = f32[1,16,256]{2,1,0:T(8,128)} async-done(((f32[1,1024,256]{2,1,0:T(8,128)}), f32[1,16,256]{2,1,0:T(8,128)}) %reduce-scatter.6.cloned.1.call-update) | async-done | bytes 16400 | tf_op jit(solution)/shard_map/reduce_scatter | solution.py:75
  (2 shorter events, 0.0 us)
Async XLA Ops:
  7.2 480.6 %reduce-scatter.4.cloned.1.call-start = ((), (), s32[]{:S(2)}) async-start(), calls=%async_computation.3 | async-start | bytes 540672 | tf_op jit(solution)/shard_map/reduce_scatter | solution.py:74
  275.1 346.3 %reduce-scatter.8.cloned.1.call-start = ((), (), s32[]{:S(2)}) async-start(), calls=%async_computation.5 | async-start | bytes 540672 | tf_op jit(solution)/shard_map/reduce_scatter | solution.py:76
  275.9 669.5 %reduce-scatter.6.cloned.1.call-start = ((), (), s32[]{:S(2)}) async-start(), calls=%async_computation.4 | async-start | bytes 1064960 | tf_op jit(solution)/shard_map/reduce_scatter | solution.py:75
Sparse Core Ops, SparseCore 0:
  275.3 212.4 reduce-scatter.3
  490.9 130.5 reduce-scatter.7
  624.5 320.9 reduce-scatter.5
where the time goes:
time: 953 us; the launch traced here: 952 us
  waiting for transfers between devices  670 us (70%)
  blocking collectives  264 us (28%)
  between operations  14.4 us (2%)
    reduce_scatter x1, waiting for transfers between devices, per_device(): lax.psum_scatter(terms_b[None], ('gx', 'gz'), scatter_dimension=1, tiled=...  324 us
    reduce_scatter x1, waiting for transfers between devices, per_device(): lax.psum_scatter(terms_a[None], ('gy', 'gz'), scatter_dimension=1, tiled=...  211 us
    all_gather x1, blocking collectives, per_device(): slab_rows_b = lax.all_gather(factor_b, ('gx', 'gz'), axis=1, tiled=True)[0]  162 us
    reduce_scatter x1, waiting for transfers between devices, per_device(): lax.psum_scatter(terms_c[None], ('gx', 'gy'), scatter_dimension=1, tiled=...  134 us
    all_gather x1, blocking collectives, per_device(): slab_rows_a = lax.all_gather(factor_a, ('gy', 'gz'), axis=1, tiled=True)[0]  65.1 us
    all_gather x1, blocking collectives, per_device(): slab_rows_c = lax.all_gather(factor_c, ('gx', 'gy'), axis=1, tiled=True)[0]  36.9 us
  transfers between devices with their start and end apart: 3, of which 3 were waited for; matrix products, arithmetic and copies ran while one was open for 0% of the time, Pallas kernels for 0%

commit v1 on v0

v1 whole, which is shorter than its diff:
```python
import functools

import jax
import jax.numpy as jnp
from jax import lax
from jax.experimental import pallas as pl
from jax.experimental.pallas import tpu as pltpu
from jax.sharding import PartitionSpec as P

R = 256
BLK = 128
SLOTS = 3
SHARD = 16
NX, NY, NZ = 2, 4, 8
CHUNK = 16
F32 = jnp.float32
BF16 = jnp.bfloat16
MESH = pl.DeviceIdType.MESH
VMEM = pl.BlockSpec(memory_space=pltpu.VMEM)


class Place:
    def __init__(self):
        gx, gy, gz = lax.axis_index("gx"), lax.axis_index("gy"), lax.axis_index("gz")
        self.y, self.x_lo = gx // 2, gx % 2
        self.x_hi, self.core = gy // 2, gy % 2
        self.z = gz

    def at(self, y=None, x_lo=None, x_hi=None, core=None, z=None):
        y = self.y if y is None else y
        x_lo = self.x_lo if x_lo is None else x_lo
        x_hi = self.x_hi if x_hi is None else x_hi
        core = self.core if core is None else core
        z = self.z if z is None else z
        return (y * 2 + x_lo, x_hi * 2 + core, z)

    def greet(self):
        barrier = pltpu.get_barrier_semaphore()
        peers = [self.at(core=1 - self.core)]
        peers += [self.at(z=(self.z + k) % NZ) for k in range(1, NZ)]
        peers += [self.at(y=(self.y + k) % NY) for k in range(1, NY)]
        peers += [self.at(x_lo=lo, x_hi=hi) for lo, hi in self.x_peers()]
        for peer in peers:
            pl.semaphore_signal(barrier, inc=1, device_id=peer, device_id_type=MESH)
        pl.semaphore_wait(barrier, len(peers))

    def x_peers(self):
        lo, hi = self.x_lo, self.x_hi
        return [(1 - lo, hi), (lo, 1 - hi), (1 - lo, 1 - hi)]


class Copies:
    def __init__(self, send_sems, recv_sems):
        self.send_sems, self.recv_sems = send_sems, recv_sems
        self.n = 0
        self.started = []

    def start(self, src, dst, peer):
        copy = pltpu.make_async_remote_copy(
            src_ref=src,
            dst_ref=dst,
            send_sem=self.send_sems.at[self.n],
            recv_sem=self.recv_sems.at[self.n],
            device_id=peer,
            device_id_type=MESH,
        )
        self.n += 1
        copy.start()
        self.started.append(copy)
        return copy

    def drain(self):
        for copy in self.started:
            copy.wait_send()


def gather_kernel(fa, fb, fc, a, b, c, send_sems, recv_sems, own_sems):
    me = Place()
    copies = Copies(send_sems, recv_sems)
    block_a = me.x_hi * 2 + me.core
    block_b = me.y * 2 + me.x_lo
    block_c = (me.x_lo * 2 + me.x_hi) * 2 + me.core
    own = [
        pltpu.make_async_copy(fa.at[0], a.at[block_a, me.z], own_sems.at[0]),
        pltpu.make_async_copy(fb.at[0], b.at[block_b, me.z], own_sems.at[1]),
        pltpu.make_async_copy(fc.at[0], c.at[me.y, block_c], own_sems.at[2]),
    ]
    for copy in own:
        copy.start()
    me.greet()
    in_a, in_b, in_c = [], [], []
    for k in range(1, NZ):
        peer = me.at(z=(me.z + k) % NZ)
        in_b.append(copies.start(fb.at[0], b.at[block_b, me.z], peer))
        in_a.append(copies.start(fa.at[0], a.at[block_a, me.z], peer))
    for k in range(1, NY):
        peer = me.at(y=(me.y + k) % NY)
        in_c.append(copies.start(fc.at[0], c.at[me.y, block_c], peer))
    for copy in own:
        copy.wait()
    for copy in in_c:
        copy.wait_recv()
    part_c = c.at[:, block_c]
    in_c = [
        copies.start(part_c, part_c, me.at(x_lo=lo, x_hi=hi)) for lo, hi in me.x_peers()
    ]
    for copy in in_b:
        copy.wait_recv()
    in_b = [copies.start(b.at[block_b], b.at[block_b], me.at(x_lo=1 - me.x_lo))]
    for copy in in_a:
        copy.wait_recv()
    in_a = [copies.start(a.at[block_a], a.at[block_a], me.at(x_hi=1 - me.x_hi))]
    for copy in in_b:
        copy.wait_recv()
    part_b = b.at[pl.ds(me.y * 2, 2)]
    in_b = [
        copies.start(part_b, part_b, me.at(y=(me.y + k) % NY)) for k in range(1, NY)
    ]
    for copy in in_c:
        copy.wait_recv()
    other = me.at(core=1 - me.core)
    in_c = []
    for x in range(4):
        part_c = c.at[:, x * 2 + me.core]
        in_c.append(copies.start(part_c, part_c, other))
    for copy in in_a:
        copy.wait_recv()
    in_a = []
    for hi in range(2):
        part_a = a.at[hi * 2 + me.core]
        in_a.append(copies.start(part_a, part_a, other))
    for copy in in_a + in_b + in_c:
        copy.wait_recv()
    copies.drain()


def gather(fa, fb, fc):
    n = 7 + 7 + 3 + 3 + 1 + 1 + 3 + 4 + 2
    a, b, c = pl.pallas_call(
        gather_kernel,
        out_shape=(
            jax.ShapeDtypeStruct((4, NZ, SHARD, R), BF16),
            jax.ShapeDtypeStruct((8, NZ, SHARD, R), BF16),
            jax.ShapeDtypeStruct((4, 8, SHARD, R), BF16),
        ),
        in_specs=[VMEM] * 3,
        out_specs=(VMEM,) * 3,
        scratch_shapes=[
            pltpu.SemaphoreType.DMA((n,)),
            pltpu.SemaphoreType.DMA((n,)),
            pltpu.SemaphoreType.DMA((3,)),
        ],
        compiler_params=pltpu.CompilerParams(collective_id=0, has_side_effects=True),
        name="gather",
    )(fa, fb, fc)
    return a.reshape(512, R), b.reshape(1024, R), c.reshape(512, R)


def terms_kernel(
    coords, filled, x_ref, m_ref, a_ref, b_ref, c_ref, ga, gb, gc, xs, acc_a, acc_c, pb, cf
):
    slot, chunk = pl.program_id(0), pl.program_id(1)

    @pl.when((slot == 0) & (chunk == 0))
    def _():
        ga[...] = jnp.zeros_like(ga)
        gb[...] = jnp.zeros_like(gb)
        gc[...] = jnp.zeros_like(gc)

    @pl.when(slot < filled[0])
    def _():
        start_a = pl.multiple_of(coords[0, slot] * BLK, BLK)
        start_b = pl.multiple_of(coords[1, slot] * BLK, BLK)
        start_c = pl.multiple_of(coords[2, slot] * BLK, BLK)

        @pl.when(chunk == 0)
        def _():
            acc_a[...] = jnp.zeros_like(acc_a)
            acc_c[...] = jnp.zeros_like(acc_c)
            cf[...] = c_ref[pl.ds(start_c, BLK), :].astype(F32)

        for u in range(BLK):
            xs[pl.ds(u, CHUNK, stride=BLK), :] = x_ref[0, u].astype(F32)
        rows_a = a_ref[pl.ds(start_a, BLK), :]
        rows_c = c_ref[pl.ds(start_c, BLK), :]
        first_b = pl.multiple_of(start_b + chunk * CHUNK, CHUNK)
        rows_b = b_ref[pl.ds(first_b, CHUNK), :].astype(F32)
        scale = pltpu.roll(m_ref[0].astype(F32) * (1.0 / BLK), (BLK - chunk * CHUNK) % BLK, 1)
        for pair in range(CHUNK // 2):
            kh, mis = [], []
            for v in (2 * pair, 2 * pair + 1):
                row = jnp.broadcast_to(rows_b[v : v + 1, :], (16, R)).astype(BF16)
                kh.append((rows_c.reshape(8, 16, R) * row[None]).reshape(BLK, R))
            kh = jnp.concatenate(kh, 0)
            log_rate = lax.dot_general(
                rows_a, kh, (((1,), (1,)), ((), ())), preferred_element_type=F32
            )
            rate = jnp.exp(log_rate)
            for j, v in enumerate((2 * pair, 2 * pair + 1)):
                x = xs[v * BLK : (v + 1) * BLK, :]
                w = scale[:, v : v + 1]
                mis.append((w * (rate[:, j * BLK : (j + 1) * BLK] - x)).astype(BF16))
            mis = jnp.concatenate(mis, 1)
            acc_a[...] += jnp.dot(mis, kh, preferred_element_type=F32)
            folded = lax.dot_general(
                mis, rows_a, (((0,), (0,)), ((), ())), preferred_element_type=F32
            )
            folded = folded.astype(BF16).astype(F32)
            f0, f1 = folded[:BLK], folded[BLK:]
            pb[2 * pair] = (f0 * cf[...]).reshape(16, 8, R).sum(0)
            pb[2 * pair + 1] = (f1 * cf[...]).reshape(16, 8, R).sum(0)
            acc_c[...] += f0 * rows_b[2 * pair : 2 * pair + 1] + f1 * rows_b[2 * pair + 1 : 2 * pair + 2]
        gb[pl.ds(first_b, CHUNK), :] += pb[...].sum(1)

        @pl.when(chunk == BLK // CHUNK - 1)
        def _():
            ga[pl.ds(start_a, BLK), :] += acc_a[...]
            gc[pl.ds(start_c, BLK), :] += acc_c[...]


def terms(blocks, fibers, coords, filled, a, b, c):
    last = BLK // CHUNK - 1

    def held(slot, filled):
        return jnp.minimum(slot, jnp.maximum(filled[0] - 1, 0))

    def x_block(slot, chunk, coords, filled):
        return (held(slot, filled), 0, jnp.where(slot < filled[0], chunk, last), 0)

    def m_block(slot, chunk, coords, filled):
        return (held(slot, filled), 0, 0)

    def whole(slot, chunk, coords, filled):
        return (0, 0)

    return pl.pallas_call(
        terms_kernel,
        out_shape=(
            jax.ShapeDtypeStruct((512, R), F32),
            jax.ShapeDtypeStruct((1024, R), F32),
            jax.ShapeDtypeStruct((512, R), F32),
        ),
        grid_spec=pltpu.PrefetchScalarGridSpec(
            num_scalar_prefetch=2,
            grid=(SLOTS, BLK // CHUNK),
            in_specs=[
                pl.BlockSpec((1, BLK, CHUNK, BLK), x_block),
                pl.BlockSpec((1, BLK, BLK), m_block),
                pl.BlockSpec((512, R), whole),
                pl.BlockSpec((1024, R), whole),
                pl.BlockSpec((512, R), whole),
            ],
            out_specs=(
                pl.BlockSpec((512, R), whole),
                pl.BlockSpec((1024, R), whole),
                pl.BlockSpec((512, R), whole),
            ),
            scratch_shapes=[
                pltpu.VMEM((CHUNK * BLK, BLK), F32),
                pltpu.VMEM((BLK, R), F32),
                pltpu.VMEM((BLK, R), F32),
                pltpu.VMEM((CHUNK, 8, R), F32),
                pltpu.VMEM((BLK, R), F32),
            ],
        ),
        name="terms",
    )(coords, filled, blocks, fibers, a, b, c)


def scatter_kernel(
    ga, gb, gc, out_a, out_b, out_c,
    a1, a2, a3, sa1, sa2, b1, b2, b3, d1, d2, d3, sb1, sb2, sd1, sd2, c1, c2, c3, sc1, sc2,
    send_sems, recv_sems,
):
    me = Place()
    copies = Copies(send_sems, recv_sems)
    me.greet()
    other = me.at(core=1 - me.core)
    left, right = slice(0, 128), slice(128, 256)
    in_b, in_d = [], []
    for k in range(1, NY):
        there = (me.y + k) % NY
        in_b.append(copies.start(gb.at[there, :, :, :, left], b1.at[k - 1], me.at(y=there)))
    to = 1 - me.x_lo
    for y in range(NY):
        in_d.append(copies.start(gb.at[y, to, :, :, right], d1.at[y], me.at(x_lo=to)))
    in_a = [
        copies.start(ga.at[hi, 1 - me.core], a1.at[hi], other) for hi in range(2)
    ]
    in_c = [copies.start(gc.at[:, 1 - me.core], c1, other)]
    for copy in in_a:
        copy.wait_recv()
    for hi in range(2):
        sa1[hi] = ga[hi, me.core] + a1[hi]
    in_a = [copies.start(sa1.at[1 - me.x_hi], a2, me.at(x_hi=1 - me.x_hi))]
    for copy in in_c:
        copy.wait_recv()
    sc1[...] = gc[:, me.core] + c1[...]
    in_c = []
    for k in range(1, NY):
        there = (me.y + k) % NY
        in_c.append(copies.start(sc1.at[pl.ds(there * 4, 4)], c2.at[k - 1], me.at(y=there)))
    for copy in in_d:
        copy.wait_recv()
    for y in range(NY):
        sd1[y] = gb[y, me.x_lo, :, :, right] + d1[y]
    in_d = []
    for k in range(1, NY):
        there = (me.y + k) % NY
        in_d.append(copies.start(sd1.at[there], d2.at[k - 1], me.at(y=there)))
    for copy in in_b:
        copy.wait_recv()
    sb1[...] = gb[me.y, :, :, :, left] + b1[0] + b1[1] + b1[2]
    in_b = [copies.start(sb1.at[to], b2, me.at(x_lo=to))]
    for copy in in_a:
        copy.wait_recv()
    sa2[...] = sa1[me.x_hi] + a2[...]
    in_a = []
    for k in range(1, NZ):
        there = (me.z + k) % NZ
        in_a.append(copies.start(sa2.at[there], a3.at[k - 1], me.at(z=there)))
    for copy in in_c:
        copy.wait_recv()
    sc2[...] = sc1[pl.ds(me.y * 4, 4)] + c2[0] + c2[1] + c2[2]
    in_c = []
    for k, (lo, hi) in enumerate(me.x_peers()):
        in_c.append(copies.start(sc2.at[lo * 2 + hi], c3.at[k], me.at(x_lo=lo, x_hi=hi)))
    for copy in in_d:
        copy.wait_recv()
    sd2[...] = sd1[me.y] + d2[0] + d2[1] + d2[2]
    in_d = []
    for k in range(1, NZ):
        there = (me.z + k) % NZ
        in_d.append(copies.start(sd2.at[there], d3.at[k - 1], me.at(z=there)))
    for copy in in_b:
        copy.wait_recv()
    sb2[...] = sb1[me.x_lo] + b2[...]
    in_b = []
    for k in range(1, NZ):
        there = (me.z + k) % NZ
        in_b.append(copies.start(sb2.at[there], b3.at[k - 1], me.at(z=there)))
    for copy in in_c:
        copy.wait_recv()
    out_c[0] = sc2[me.x_lo * 2 + me.x_hi] + c3[0] + c3[1] + c3[2]
    for copy in in_a:
        copy.wait_recv()
    out_a[0] = sa2[me.z] + a3[...].sum(0)
    for copy in in_d:
        copy.wait_recv()
    out_b[0, :, right] = sd2[me.z] + d3[...].sum(0)
    for copy in in_b:
        copy.wait_recv()
    out_b[0, :, left] = sb2[me.z] + b3[...].sum(0)
    copies.drain()


def scatter(ga, gb, gc):
    n = 3 + 4 + 2 + 1 + 1 + 3 + 3 + 1 + 7 + 3 + 7 + 7
    half = R // 2

    def buf(*shape):
        return pltpu.VMEM(shape, F32)

    return pl.pallas_call(
        scatter_kernel,
        out_shape=(jax.ShapeDtypeStruct((1, SHARD, R), F32),) * 3,
        in_specs=[VMEM] * 3,
        out_specs=(VMEM,) * 3,
        scratch_shapes=[
            buf(2, NZ, SHARD, R), buf(NZ, SHARD, R), buf(7, SHARD, R),
            buf(2, NZ, SHARD, R), buf(NZ, SHARD, R),
            buf(3, 2, NZ, SHARD, half), buf(NZ, SHARD, half), buf(7, SHARD, half),
            buf(4, NZ, SHARD, half), buf(3, NZ, SHARD, half), buf(7, SHARD, half),
            buf(2, NZ, SHARD, half), buf(NZ, SHARD, half),
            buf(4, NZ, SHARD, half), buf(NZ, SHARD, half),
            buf(16, SHARD, R), buf(3, 4, SHARD, R), buf(3, SHARD, R),
            buf(16, SHARD, R), buf(4, SHARD, R),
            pltpu.SemaphoreType.DMA((n,)),
            pltpu.SemaphoreType.DMA((n,)),
        ],
        compiler_params=pltpu.CompilerParams(collective_id=1, has_side_effects=True),
        name="scatter",
    )(
        ga.reshape(2, 2, NZ, SHARD, R),
        gb.reshape(NY, 2, NZ, SHARD, R),
        gc.reshape(16, 2, SHARD, R),
    )


def per_device(tensor_blocks, fiber_mask, block_coords, block_counts, factor_a, factor_b, factor_c):
    a, b, c = gather(factor_a, factor_b, factor_c)
    ga, gb, gc = terms(
        tensor_blocks.reshape(SLOTS, BLK, BLK, BLK),
        fiber_mask.reshape(SLOTS, BLK, BLK),
        block_coords.reshape(3, SLOTS),
        block_counts.reshape(1),
        a, b, c,
    )
    return scatter(ga, gb, gc)


def solution(mesh):
    placed = (
        P("gx", "gy", "gz", None, None, None, None),
        P("gx", "gy", "gz", None, None, None),
        P("gx", "gy", "gz", None, None),
        P("gx", "gy", "gz"),
        P("gx", ("gy", "gz"), None),
        P("gy", ("gx", "gz"), None),
        P("gz", ("gx", "gy"), None),
    )
    return jax.shard_map(
        per_device,
        mesh=mesh,
        in_specs=placed,
        out_specs=(
            P("gx", ("gy", "gz"), None),
            P("gy", ("gx", "gz"), None),
            P("gz", ("gx", "gy"), None),
        ),
        check_vma=False,
    )
```

time: 953 us -> 118 us (0.12)
  waiting for transfers between devices: 670 us -> 0 us
  blocking collectives: 264 us -> 0 us
  Pallas kernels: 0 us -> 111 us
  between operations: 14.4 us -> 1.3 us
    reduce_scatter x3 -> x0, waiting for transfers between devices: 669 us -> none  [the longest x1 324 us: per_device(): lax.psum_scatter(terms_b[None], ('gx', 'gz'), scatter_dimension=1, tiled=...]
    all_gather x3 -> x0, blocking collectives: 264 us -> none  [the longest x1 162 us: per_device(): slab_rows_b = lax.all_gather(factor_b, ('gx', 'gz'), axis=1, tiled=True)[0]]
    pallas_call x0 -> x3, Pallas kernels: none -> 111 us  [the longest x1 80.1 us: scatter(): pl.pallas_call(scatter_kernel, out_shape=(jax.ShapeDtypeStruct((1, SHARD,...]
  transfers between devices with their start and end apart: 3 -> 0, of which waited for: 3 -> 0; matrix products, arithmetic and copies ran while one was open for 0% -> 0% of each run, Pallas kernels for 0% -> 0%
where the time goes in v1:
time: 118 us; the launch traced here: 117 us
  Pallas kernels  111 us (94%)
  local copies, waits for them, and re-layouts  5.23 us (4%)
  between operations  1.3 us (1%)
    pallas_call x1, Pallas kernels, scatter(): pl.pallas_call(scatter_kernel, out_shape=(jax.ShapeDtypeStruct((1, SHARD,...  80.1 us
    pallas_call x1, Pallas kernels, gather(): pl.pallas_call(gather_kernel, out_shape=(jax.ShapeDtypeStruct((4, NZ, SHA...  25.5 us
    pallas_call x1, Pallas kernels, terms(): pl.pallas_call(terms_kernel, out_shape=(jax.ShapeDtypeStruct((512, R), F3...  5.4 us
    unnamed x4, local copies, waits for them, and re-layouts  5.23 us

profile of v1, /device:TPU:4, one launch (start us, length us, event | category | flops | bytes accessed | tf_op | source)
XLA Modules:
  0.0 117.5 jit_solution(8157754325459516704)
XLA Ops:
  1.3 1.3 %copy.12 = s32[1,1,1,3,3]{4,3,2,1,0:T(4,128)} copy(s32[1,1,1,3,3]{4,2,3,1,0:T(1,128)} %param.9) | data formatting | bytes 72
  2.5 25.5 %gather.1 = (bf16[4,8,16,256]{3,2,1,0:T(8,128)(2,1)}, bf16[8,8,16,256]{3,2,1,0:T(8,128)(2,1)}, bf16[4,8,16,256]{3,2,1,0:T(8,128)(2,1)}) custom-call(bf16[1,16,256]{2,1,0:T(8,128)(2,1)} %fa.1, bf16[1,16,256]{2,1,0:T(8,128)(2,1)} %fb.1, bf16[1,16,256]{2,1,0:T(8,128)(2,1)} %fc.1), custom_call_target="tpu_custom_call" | custom-call | tf_op jit(solution)/shard_map/gather/pallas_call | solution.py:139
  28.0 5.4 %terms.1 = (f32[512,256]{1,0:T(8,128)}, f32[1024,256]{1,0:T(8,128)}, f32[512,256]{1,0:T(8,128)}) custom-call(s32[3,3]{1,0:T(4,128)} %bitcast.21, s32[1]{0:T(128)} %bitcast.12.filled, bf16[3,128,128,128]{3,2,1,0:T(8,128)(2,1)} %bitcast.13, s32[3,128,128]{2,1,0:T(8,128)} %bitcast.20, bf16[512,256]{1,0:T(8,128)(2,1)} %bitcast.18, bf16[1024,256]{1,0:T(8,128)(2,1)} %bitcast.15, ...), custom_call_target="tpu_custom_call" | custom-call | tf_op jit(solution)/shard_map/terms/pallas_call | solution.py:236
  33.4 80.1 %scatter.1 = (f32[1,16,256]{2,1,0:T(8,128)}, f32[1,16,256]{2,1,0:T(8,128)}, f32[1,16,256]{2,1,0:T(8,128)}) custom-call(f32[2,2,8,16,256]{4,3,2,1,0:T(8,128)} %bitcast.16, f32[4,2,8,16,256]{4,3,2,1,0:T(8,128)} %bitcast.14, f32[16,2,16,256]{3,2,1,0:T(8,128)} %bitcast.17), custom_call_target="tpu_custom_call" | custom-call | tf_op jit(solution)/shard_map/scatter/pallas_call | solution.py:364
  113.5 1.3 %copy.17 = f32[1,16,256]{2,1,0:T(8,128)} copy(f32[1,16,256]{2,1,0:T(8,128)} %get-tuple-element.18) | data formatting | bytes 32768
  114.8 1.3 %copy.18 = f32[1,16,256]{2,1,0:T(8,128)} copy(f32[1,16,256]{2,1,0:T(8,128)} %get-tuple-element.19) | data formatting | bytes 32768
  116.2 1.3 %copy.19 = f32[1,16,256]{2,1,0:T(8,128)} copy(f32[1,16,256]{2,1,0:T(8,128)} %get-tuple-element.20) | data formatting | bytes 32768

commit v2 on v1

--- a/solution.py
+++ b/solution.py
@@ -157,7 +157,7 @@
 
 
 def terms_kernel(
-    coords, filled, x_ref, m_ref, a_ref, b_ref, c_ref, ga, gb, gc, xs, acc_a, acc_c, pb, cf
+    coords, filled, x_ref, m_ref, a_ref, b_ref, c_ref, ga, gb, gc, xs, acc_a, acc_c, pb, cf, perm, kh_s, mis_s
 ):
     slot, chunk = pl.program_id(0), pl.program_id(1)
 
@@ -166,12 +166,16 @@
         ga[...] = jnp.zeros_like(ga)
         gb[...] = jnp.zeros_like(gb)
         gc[...] = jnp.zeros_like(gc)
+        row = lax.broadcasted_iota(jnp.int32, (256, 256), 0)
+        col = lax.broadcasted_iota(jnp.int32, (256, 256), 1)
+        swapped = (row % 16) * 16 + row // 16
+        perm[...] = jnp.where(col == swapped, 1.0, 0.0).astype(BF16)
 
     @pl.when(slot < filled[0])
     def _():
-        start_a = pl.multiple_of(coords[0, slot] * BLK, BLK)
-        start_b = pl.multiple_of(coords[1, slot] * BLK, BLK)
-        start_c = pl.multiple_of(coords[2, slot] * BLK, BLK)
+        start_a = pl.multiple_of(coords[0, 0, slot] * BLK, BLK)
+        start_b = pl.multiple_of(coords[1, 0, slot] * BLK, BLK)
+        start_c = pl.multiple_of(coords[2, 0, slot] * BLK, BLK)
 
         @pl.when(chunk == 0)
         def _():
@@ -179,8 +183,10 @@
             acc_c[...] = jnp.zeros_like(acc_c)
             cf[...] = c_ref[pl.ds(start_c, BLK), :].astype(F32)
 
-        for u in range(BLK):
-            xs[pl.ds(u, CHUNK, stride=BLK), :] = x_ref[0, u].astype(F32)
+        for g in range(BLK // 16):
+            xg = x_ref[0, 16 * g : 16 * g + 16].reshape(256, BLK)
+            xg = jnp.dot(perm[...], xg, preferred_element_type=F32)
+            xs[:, 16 * g : 16 * g + 16, :] = xg.reshape(16, 16, BLK)
         rows_a = a_ref[pl.ds(start_a, BLK), :]
         rows_c = c_ref[pl.ds(start_c, BLK), :]
         first_b = pl.multiple_of(start_b + chunk * CHUNK, CHUNK)
@@ -192,16 +198,17 @@
                 row = jnp.broadcast_to(rows_b[v : v + 1, :], (16, R)).astype(BF16)
                 kh.append((rows_c.reshape(8, 16, R) * row[None]).reshape(BLK, R))
             kh = jnp.concatenate(kh, 0)
+            kh_s[256 * pair : 256 * pair + 256, :] = kh
             log_rate = lax.dot_general(
                 rows_a, kh, (((1,), (1,)), ((), ())), preferred_element_type=F32
             )
             rate = jnp.exp(log_rate)
             for j, v in enumerate((2 * pair, 2 * pair + 1)):
-                x = xs[v * BLK : (v + 1) * BLK, :]
+                x = xs[v]
                 w = scale[:, v : v + 1]
                 mis.append((w * (rate[:, j * BLK : (j + 1) * BLK] - x)).astype(BF16))
             mis = jnp.concatenate(mis, 1)
-            acc_a[...] += jnp.dot(mis, kh, preferred_element_type=F32)
+            mis_s[:, 256 * pair : 256 * pair + 256] = mis
             folded = lax.dot_general(
                 mis, rows_a, (((0,), (0,)), ((), ())), preferred_element_type=F32
             )
@@ -210,6 +217,7 @@
             pb[2 * pair] = (f0 * cf[...]).reshape(16, 8, R).sum(0)
             pb[2 * pair + 1] = (f1 * cf[...]).reshape(16, 8, R).sum(0)
             acc_c[...] += f0 * rows_b[2 * pair : 2 * pair + 1] + f1 * rows_b[2 * pair + 1 : 2 * pair + 2]
+        acc_a[...] += jnp.dot(mis_s[...], kh_s[...], preferred_element_type=F32)
         gb[pl.ds(first_b, CHUNK), :] += pb[...].sum(1)
 
         @pl.when(chunk == BLK // CHUNK - 1)
@@ -256,11 +264,14 @@
                 pl.BlockSpec((512, R), whole),
             ),
             scratch_shapes=[
-                pltpu.VMEM((CHUNK * BLK, BLK), F32),
+                pltpu.VMEM((CHUNK, BLK, BLK), F32),
                 pltpu.VMEM((BLK, R), F32),
                 pltpu.VMEM((BLK, R), F32),
                 pltpu.VMEM((CHUNK, 8, R), F32),
                 pltpu.VMEM((BLK, R), F32),
+                pltpu.VMEM((256, 256), BF16),
+                pltpu.VMEM((CHUNK * BLK, R), BF16),
+                pltpu.VMEM((BLK, CHUNK * BLK), BF16),
             ],
         ),
         name="terms",
@@ -268,7 +279,7 @@
 
 
 def scatter_kernel(
-    ga, gb, gc, out_a, out_b, out_c,
+    ga, gb, gc, out,
     a1, a2, a3, sa1, sa2, b1, b2, b3, d1, d2, d3, sb1, sb2, sd1, sd2, c1, c2, c3, sc1, sc2,
     send_sems, recv_sems,
 ):
@@ -341,16 +352,16 @@
         in_b.append(copies.start(sb2.at[there], b3.at[k - 1], me.at(z=there)))
     for copy in in_c:
         copy.wait_recv()
-    out_c[0] = sc2[me.x_lo * 2 + me.x_hi] + c3[0] + c3[1] + c3[2]
+    out[2] = sc2[me.x_lo * 2 + me.x_hi] + c3[0] + c3[1] + c3[2]
     for copy in in_a:
         copy.wait_recv()
-    out_a[0] = sa2[me.z] + a3[...].sum(0)
+    out[0] = sa2[me.z] + a3[...].sum(0)
     for copy in in_d:
         copy.wait_recv()
-    out_b[0, :, right] = sd2[me.z] + d3[...].sum(0)
+    out[1, :, right] = sd2[me.z] + d3[...].sum(0)
     for copy in in_b:
         copy.wait_recv()
-    out_b[0, :, left] = sb2[me.z] + b3[...].sum(0)
+    out[1, :, left] = sb2[me.z] + b3[...].sum(0)
     copies.drain()
 
 
@@ -361,11 +372,11 @@
     def buf(*shape):
         return pltpu.VMEM(shape, F32)
 
-    return pl.pallas_call(
+    out = pl.pallas_call(
         scatter_kernel,
-        out_shape=(jax.ShapeDtypeStruct((1, SHARD, R), F32),) * 3,
+        out_shape=jax.ShapeDtypeStruct((3, SHARD, R), F32),
         in_specs=[VMEM] * 3,
-        out_specs=(VMEM,) * 3,
+        out_specs=VMEM,
         scratch_shapes=[
             buf(2, NZ, SHARD, R), buf(NZ, SHARD, R), buf(7, SHARD, R),
             buf(2, NZ, SHARD, R), buf(NZ, SHARD, R),
@@ -385,6 +396,18 @@
         gb.reshape(NY, 2, NZ, SHARD, R),
         gc.reshape(16, 2, SHARD, R),
     )
+    return pl.pallas_call(
+        part_kernel,
+        out_shape=(jax.ShapeDtypeStruct((1, SHARD, R), F32),) * 3,
+        in_specs=[VMEM],
+        out_specs=(VMEM,) * 3,
+        name="part",
+    )(out)
+
+
+def part_kernel(rows, a, b, c):
+    for i, ref in enumerate((a, b, c)):
+        ref[0] = rows[i]
 
 
 def per_device(tensor_blocks, fiber_mask, block_coords, block_counts, factor_a, factor_b, factor_c):
@@ -392,7 +415,7 @@
     ga, gb, gc = terms(
         tensor_blocks.reshape(SLOTS, BLK, BLK, BLK),
         fiber_mask.reshape(SLOTS, BLK, BLK),
-        block_coords.reshape(3, SLOTS),
+        block_coords.reshape(3, 1, SLOTS),
         block_counts.reshape(1),
         a, b, c,
     )

time: 118 us -> 93.3 us (0.79)
  Pallas kernels: 111 us -> 91.4 us
  local copies, waits for them, and re-layouts: 5.23 us -> 0 us
    pallas_call x1 -> x2, Pallas kernels: 80.1 us -> 36.4 us  [the longest x1 35 us: scatter(): pl.pallas_call(scatter_kernel, out_shape=jax.ShapeDtypeStruct((3, SHARD,...]
    pallas_call x1, Pallas kernels: 5.4 us -> 29.5 us  [terms(): pl.pallas_call(terms_kernel, out_shape=(jax.ShapeDtypeStruct((512, R), F3...]
    unnamed x4 -> x0, local copies, waits for them, and re-layouts: 5.23 us -> none
where the time goes in v2:
time: 93.3 us; the launch traced here: 92.7 us
  Pallas kernels  91.4 us (98%)
  between operations  1.29 us (1%)
    pallas_call x1, Pallas kernels, scatter(): pl.pallas_call(scatter_kernel, out_shape=jax.ShapeDtypeStruct((3, SHARD,...  35 us
    pallas_call x1, Pallas kernels, terms(): pl.pallas_call(terms_kernel, out_shape=(jax.ShapeDtypeStruct((512, R), F3...  29.5 us
    pallas_call x1, Pallas kernels, gather(): pl.pallas_call(gather_kernel, out_shape=(jax.ShapeDtypeStruct((4, NZ, SHA...  25.6 us

profile of v2, /device:TPU:4, one launch (start us, length us, event | category | flops | bytes accessed | tf_op | source)
XLA Modules:
  0.0 92.7 jit_solution(2950881264639474459)
XLA Ops:
  1.3 25.6 %gather.1 = (bf16[4,8,16,256]{3,2,1,0:T(8,128)(2,1)}, bf16[8,8,16,256]{3,2,1,0:T(8,128)(2,1)}, bf16[4,8,16,256]{3,2,1,0:T(8,128)(2,1)}) custom-call(bf16[1,16,256]{2,1,0:T(8,128)(2,1)} %fa.1, bf16[1,16,256]{2,1,0:T(8,128)(2,1)} %fb.1, bf16[1,16,256]{2,1,0:T(8,128)(2,1)} %fc.1), custom_call_target="tpu_custom_call" | custom-call | tf_op jit(solution)/shard_map/gather/pallas_call | solution.py:139
  26.9 29.5 %terms.1 = (f32[512,256]{1,0:T(8,128)}, f32[1024,256]{1,0:T(8,128)}, f32[512,256]{1,0:T(8,128)}) custom-call(s32[3,1,3]{2,1,0:T(1,128)} %bitcast.19, s32[1]{0:T(128)} %bitcast.10.filled, bf16[3,128,128,128]{3,2,1,0:T(8,128)(2,1)} %bitcast.11, s32[3,128,128]{2,1,0:T(8,128)} %bitcast.18, bf16[512,256]{1,0:T(8,128)(2,1)} %bitcast.16, ...), custom_call_target="tpu_custom_call" | custom-call | tf_op jit(solution)/shard_map/terms/pallas_call | solution.py:244
  56.3 35.0 %scatter.1.rows = f32[3,16,256]{2,1,0:T(8,128)} custom-call(f32[2,2,8,16,256]{4,3,2,1,0:T(8,128)} %bitcast.14, f32[4,2,8,16,256]{4,3,2,1,0:T(8,128)} %bitcast.12, f32[16,2,16,256]{3,2,1,0:T(8,128)} %bitcast.15), custom_call_target="tpu_custom_call" | custom-call | tf_op jit(solution)/shard_map/scatter/pallas_call | solution.py:375
  91.3 1.4 %part.1 = (f32[1,16,256]{2,1,0:T(8,128)}, f32[1,16,256]{2,1,0:T(8,128)}, f32[1,16,256]{2,1,0:T(8,128)}) custom-call(f32[3,16,256]{2,1,0:T(8,128)} %scatter.1.rows), custom_call_target="tpu_custom_call" | custom-call | tf_op jit(solution)/shard_map/part/pallas_call | solution.py:399

commit v3 on v2

--- a/solution.py
+++ b/solution.py
@@ -13,6 +13,9 @@
 SHARD = 16
 NX, NY, NZ = 2, 4, 8
 CHUNK = 16
+CHUNKS = BLK // CHUNK
+NV = 8
+UNIT = 8
 F32 = jnp.float32
 BF16 = jnp.bfloat16
 MESH = pl.DeviceIdType.MESH
@@ -42,7 +45,10 @@
         peers += [self.at(x_lo=lo, x_hi=hi) for lo, hi in self.x_peers()]
         for peer in peers:
             pl.semaphore_signal(barrier, inc=1, device_id=peer, device_id_type=MESH)
-        pl.semaphore_wait(barrier, len(peers))
+        self.greeted = len(peers)
+
+    def met(self):
+        pl.semaphore_wait(pltpu.get_barrier_semaphore(), self.greeted)
 
     def x_peers(self):
         lo, hi = self.x_lo, self.x_hi
@@ -74,90 +80,178 @@
             copy.wait_send()
 
 
-def gather_kernel(fa, fb, fc, a, b, c, send_sems, recv_sems, own_sems):
+def turn_chunks(lo, hi, x, xt, xin, xout, perm, in_sems, out_sems):
+    def source(i):
+        return x.at[i // CHUNKS, :, pl.ds(pl.multiple_of(i % CHUNKS * CHUNK, CHUNK), CHUNK), :]
+
+    def load(i):
+        return pltpu.make_async_copy(source(i), xin.at[i % 2], in_sems.at[i % 2])
+
+    def store(i):
+        return pltpu.make_async_copy(xout.at[i % 2], xt.at[i], out_sems.at[i % 2])
+
+    if lo == 0:
+        load(0).start()
+
+    def body(i, carry):
+        load(i).wait()
+
+        @pl.when(i < SLOTS * CHUNKS - 1)
+        def _():
+            load(i + 1).start()
+
+        @pl.when(i >= 2)
+        def _():
+            store(i - 2).wait()
+
+        for g in range(BLK // UNIT):
+            us = slice(UNIT * g, UNIT * g + UNIT)
+            rows = xin[i % 2, us].reshape(UNIT * CHUNK, BLK)
+            rows = jnp.dot(perm[...], rows, preferred_element_type=F32).astype(BF16)
+            xout[i % 2, :, us, :] = rows.reshape(CHUNK, UNIT, BLK)
+        store(i).start()
+        return carry
+
+    lax.fori_loop(lo, hi, body, 0)
+    if hi == SLOTS * CHUNKS:
+        store(hi - 2).wait()
+        store(hi - 1).wait()
+
+
+NEAR = (0, 7, 1, 6, 2, 5, 3, 4)
+
+
+def gather_kernel(
+    fa, fb, fc, x, a, b, c, xt, xin, xout, perm, send_sems, recv_sems, own_sems, in_sems, out_sems
+):
     me = Place()
     copies = Copies(send_sems, recv_sems)
+    turn = functools.partial(
+        turn_chunks, x=x, xt=xt, xin=xin, xout=xout, perm=perm, in_sems=in_sems, out_sems=out_sems
+    )
     block_a = me.x_hi * 2 + me.core
     block_b = me.y * 2 + me.x_lo
     block_c = (me.x_lo * 2 + me.x_hi) * 2 + me.core
+    me.greet()
     own = [
-        pltpu.make_async_copy(fa.at[0], a.at[block_a, me.z], own_sems.at[0]),
-        pltpu.make_async_copy(fb.at[0], b.at[block_b, me.z], own_sems.at[1]),
+        pltpu.make_async_copy(fb.at[0], b.at[block_b, me.z], own_sems.at[0]),
+        pltpu.make_async_copy(fa.at[0], a.at[block_a, me.z], own_sems.at[1]),
         pltpu.make_async_copy(fc.at[0], c.at[me.y, block_c], own_sems.at[2]),
     ]
     for copy in own:
         copy.start()
-    me.greet()
-    in_a, in_b, in_c = [], [], []
-    for k in range(1, NZ):
-        peer = me.at(z=(me.z + k) % NZ)
-        in_b.append(copies.start(fb.at[0], b.at[block_b, me.z], peer))
-        in_a.append(copies.start(fa.at[0], a.at[block_a, me.z], peer))
+    row = lax.broadcasted_iota(jnp.int32, perm.shape, 0)
+    col = lax.broadcasted_iota(jnp.int32, perm.shape, 1)
+    swapped = (row % UNIT) * CHUNK + row // UNIT
+    perm[...] = jnp.where(col == swapped, 1.0, 0.0).astype(BF16)
+    turn(0, 4)
+    me.met()
+    z_b, z_a, y_c = {}, {}, []
+    for k in reversed(NEAR[1:]):
+        z_b[k] = copies.start(fb.at[0], b.at[block_b, me.z], me.at(z=(me.z + k) % NZ))
     for k in range(1, NY):
-        peer = me.at(y=(me.y + k) % NY)
-        in_c.append(copies.start(fc.at[0], c.at[me.y, block_c], peer))
+        y_c.append(copies.start(fc.at[0], c.at[me.y, block_c], me.at(y=(me.y + k) % NY)))
+    for k in reversed(NEAR[1:]):
+        z_a[k] = copies.start(fa.at[0], a.at[block_a, me.z], me.at(z=(me.z + k) % NZ))
+    up, down = me.at(y=(me.y + 1) % NY), me.at(y=(me.y + NY - 1) % NY)
+    above, below = (me.y + 1) % NY, (me.y + NY - 1) % NY
+    beside = me.at(x_lo=1 - me.x_lo)
+
+    def piece(y, x_lo, k):
+        return b.at[y * 2 + x_lo, (me.z + NZ - k) % NZ]
+
+    def send(ref, peer):
+        return copies.start(ref, ref, peer)
+
     for copy in own:
         copy.wait()
-    for copy in in_c:
+    to_x, to_up, to_down = {}, {}, {}
+
+    def spread(k):
+        if k:
+            z_b[k].wait_recv()
+        ref = piece(me.y, me.x_lo, k)
+        to_x[k] = send(ref, beside)
+        to_up[0, k] = send(ref, up)
+        to_down[0, k] = send(ref, down)
+
+    spread(0)
+    turn(4, 10)
+    for k in NEAR[1:]:
+        spread(k)
+    for copy in y_c:
         copy.wait_recv()
     part_c = c.at[:, block_c]
-    in_c = [
-        copies.start(part_c, part_c, me.at(x_lo=lo, x_hi=hi)) for lo, hi in me.x_peers()
-    ]
-    for copy in in_b:
-        copy.wait_recv()
-    in_b = [copies.start(b.at[block_b], b.at[block_b], me.at(x_lo=1 - me.x_lo))]
-    for copy in in_a:
-        copy.wait_recv()
-    in_a = [copies.start(a.at[block_a], a.at[block_a], me.at(x_hi=1 - me.x_hi))]
-    for copy in in_b:
-        copy.wait_recv()
-    part_b = b.at[pl.ds(me.y * 2, 2)]
-    in_b = [
-        copies.start(part_b, part_b, me.at(y=(me.y + k) % NY)) for k in range(1, NY)
-    ]
-    for copy in in_c:
-        copy.wait_recv()
+    x_c = [send(part_c, me.at(x_lo=lo, x_hi=hi)) for lo, hi in me.x_peers()]
     other = me.at(core=1 - me.core)
-    in_c = []
-    for x in range(4):
-        part_c = c.at[:, x * 2 + me.core]
-        in_c.append(copies.start(part_c, part_c, other))
-    for copy in in_a:
-        copy.wait_recv()
-    in_a = []
-    for hi in range(2):
-        part_a = a.at[hi * 2 + me.core]
-        in_a.append(copies.start(part_a, part_a, other))
-    for copy in in_a + in_b + in_c:
+    for k in NEAR[1:]:
+        z_a[k].wait_recv()
+    x_a = send(a.at[block_a], me.at(x_hi=1 - me.x_hi))
+    core_a = [send(a.at[block_a], other)]
+    turn(10, 14)
+    for k in NEAR:
+        to_x[k].wait_recv()
+        ref = piece(me.y, 1 - me.x_lo, k)
+        to_up[1, k] = send(ref, up)
+        to_down[1, k] = send(ref, down)
+    turn(14, 18)
+    relayed = []
+    for side in range(2):
+        x_lo = me.x_lo if side == 0 else 1 - me.x_lo
+        for k in NEAR:
+            to_up[side, k].wait_recv()
+            to_down[side, k].wait_recv()
+            if k % 2 == 0:
+                relayed.append(send(piece(below, x_lo, k), up))
+            else:
+                relayed.append(send(piece(above, x_lo, k), down))
+        if side == 0:
+            for copy in x_c:
+                copy.wait_recv()
+            core_c = []
+            for lo_hi in range(4):
+                core_c.append(send(c.at[:, lo_hi * 2 + me.core], other))
+            x_a.wait_recv()
+            core_a.append(send(a.at[(1 - me.x_hi) * 2 + me.core], other))
+            turn(18, 22)
+    turn(22, 24)
+    for copy in core_a + core_c + relayed:
         copy.wait_recv()
     copies.drain()
 
 
-def gather(fa, fb, fc):
-    n = 7 + 7 + 3 + 3 + 1 + 1 + 3 + 4 + 2
-    a, b, c = pl.pallas_call(
+def gather(fa, fb, fc, x):
+    n = 7 + 7 + 3 + 8 * 3 + 3 + 2 + 8 * 2 + 16 + 4 + 1
+    a, b, c, xt = pl.pallas_call(
         gather_kernel,
         out_shape=(
             jax.ShapeDtypeStruct((4, NZ, SHARD, R), BF16),
             jax.ShapeDtypeStruct((8, NZ, SHARD, R), BF16),
             jax.ShapeDtypeStruct((4, 8, SHARD, R), BF16),
+            jax.ShapeDtypeStruct((SLOTS * CHUNKS, CHUNK, BLK, BLK), BF16),
         ),
-        in_specs=[VMEM] * 3,
-        out_specs=(VMEM,) * 3,
+        in_specs=[VMEM] * 3 + [pl.BlockSpec(memory_space=pl.ANY)],
+        out_specs=(VMEM,) * 3 + (pl.BlockSpec(memory_space=pl.ANY),),
         scratch_shapes=[
+            pltpu.VMEM((2, BLK, CHUNK, BLK), BF16),
+            pltpu.VMEM((2, CHUNK, BLK, BLK), BF16),
+            pltpu.VMEM((UNIT * CHUNK, UNIT * CHUNK), BF16),
             pltpu.SemaphoreType.DMA((n,)),
             pltpu.SemaphoreType.DMA((n,)),
             pltpu.SemaphoreType.DMA((3,)),
+            pltpu.SemaphoreType.DMA((2,)),
+            pltpu.SemaphoreType.DMA((2,)),
         ],
         compiler_params=pltpu.CompilerParams(collective_id=0, has_side_effects=True),
         name="gather",
-    )(fa, fb, fc)
-    return a.reshape(512, R), b.reshape(1024, R), c.reshape(512, R)
+    )(fa, fb, fc, x)
+    return (
+        a.reshape(512, R), b.reshape(1024, R), c.reshape(512, R), xt.reshape(SLOTS, BLK, BLK, BLK)
+    )
 
 
 def terms_kernel(
-    coords, filled, x_ref, m_ref, a_ref, b_ref, c_ref, ga, gb, gc, xs, acc_a, acc_c, pb, cf, perm, kh_s, mis_s
+    coords, filled, x_ref, m_ref, a_ref, b_ref, c_ref, ga, gb, gc, acc_a, acc_c, pb, cf, kh_s, mis_s
 ):
     slot, chunk = pl.program_id(0), pl.program_id(1)
 
@@ -166,10 +260,6 @@
         ga[...] = jnp.zeros_like(ga)
         gb[...] = jnp.zeros_like(gb)
         gc[...] = jnp.zeros_like(gc)
-        row = lax.broadcasted_iota(jnp.int32, (256, 256), 0)
-        col = lax.broadcasted_iota(jnp.int32, (256, 256), 1)
-        swapped = (row % 16) * 16 + row // 16
-        perm[...] = jnp.where(col == swapped, 1.0, 0.0).astype(BF16)
 
     @pl.when(slot < filled[0])
     def _():
@@ -183,57 +273,55 @@
             acc_c[...] = jnp.zeros_like(acc_c)
             cf[...] = c_ref[pl.ds(start_c, BLK), :].astype(F32)
 
-        for g in range(BLK // 16):
-            xg = x_ref[0, 16 * g : 16 * g + 16].reshape(256, BLK)
-            xg = jnp.dot(perm[...], xg, preferred_element_type=F32)
-            xs[:, 16 * g : 16 * g + 16, :] = xg.reshape(16, 16, BLK)
         rows_a = a_ref[pl.ds(start_a, BLK), :]
         rows_c = c_ref[pl.ds(start_c, BLK), :]
         first_b = pl.multiple_of(start_b + chunk * CHUNK, CHUNK)
         rows_b = b_ref[pl.ds(first_b, CHUNK), :].astype(F32)
         scale = pltpu.roll(m_ref[0].astype(F32) * (1.0 / BLK), (BLK - chunk * CHUNK) % BLK, 1)
-        for pair in range(CHUNK // 2):
+        for first in range(0, CHUNK, NV):
+            vs = range(first, first + NV)
             kh, mis = [], []
-            for v in (2 * pair, 2 * pair + 1):
+            for v in vs:
                 row = jnp.broadcast_to(rows_b[v : v + 1, :], (16, R)).astype(BF16)
                 kh.append((rows_c.reshape(8, 16, R) * row[None]).reshape(BLK, R))
             kh = jnp.concatenate(kh, 0)
-            kh_s[256 * pair : 256 * pair + 256, :] = kh
+            kh_s[BLK * first : BLK * (first + NV), :] = kh
             log_rate = lax.dot_general(
                 rows_a, kh, (((1,), (1,)), ((), ())), preferred_element_type=F32
             )
             rate = jnp.exp(log_rate)
-            for j, v in enumerate((2 * pair, 2 * pair + 1)):
-                x = xs[v]
+            for j, v in enumerate(vs):
+                x = x_ref[0, v].astype(F32)
                 w = scale[:, v : v + 1]
                 mis.append((w * (rate[:, j * BLK : (j + 1) * BLK] - x)).astype(BF16))
             mis = jnp.concatenate(mis, 1)
-            mis_s[:, 256 * pair : 256 * pair + 256] = mis
+            mis_s[:, BLK * first : BLK * (first + NV)] = mis
             folded = lax.dot_general(
                 mis, rows_a, (((0,), (0,)), ((), ())), preferred_element_type=F32
             )
             folded = folded.astype(BF16).astype(F32)
-            f0, f1 = folded[:BLK], folded[BLK:]
-            pb[2 * pair] = (f0 * cf[...]).reshape(16, 8, R).sum(0)
-            pb[2 * pair + 1] = (f1 * cf[...]).reshape(16, 8, R).sum(0)
-            acc_c[...] += f0 * rows_b[2 * pair : 2 * pair + 1] + f1 * rows_b[2 * pair + 1 : 2 * pair + 2]
+            total = None
+            for j, v in enumerate(vs):
+                f = folded[j * BLK : (j + 1) * BLK]
+                pb[v] = (f * cf[...]).reshape(16, 8, R).sum(0)
+                part = f * rows_b[v : v + 1]
+                total = part if total is None else total + part
+            acc_c[...] += total
         acc_a[...] += jnp.dot(mis_s[...], kh_s[...], preferred_element_type=F32)
         gb[pl.ds(first_b, CHUNK), :] += pb[...].sum(1)
 
-        @pl.when(chunk == BLK // CHUNK - 1)
+        @pl.when(chunk == CHUNKS - 1)
         def _():
             ga[pl.ds(start_a, BLK), :] += acc_a[...]
             gc[pl.ds(start_c, BLK), :] += acc_c[...]
 
 
 def terms(blocks, fibers, coords, filled, a, b, c):
-    last = BLK // CHUNK - 1
-
     def held(slot, filled):
         return jnp.minimum(slot, jnp.maximum(filled[0] - 1, 0))
 
     def x_block(slot, chunk, coords, filled):
-        return (held(slot, filled), 0, jnp.where(slot < filled[0], chunk, last), 0)
+        return (held(slot, filled), jnp.where(slot < filled[0], chunk, CHUNKS - 1), 0, 0)
 
     def m_block(slot, chunk, coords, filled):
         return (held(slot, filled), 0, 0)
@@ -250,9 +338,9 @@
         ),
         grid_spec=pltpu.PrefetchScalarGridSpec(
             num_scalar_prefetch=2,
-            grid=(SLOTS, BLK // CHUNK),
+            grid=(SLOTS, CHUNKS),
             in_specs=[
-                pl.BlockSpec((1, BLK, CHUNK, BLK), x_block),
+                pl.BlockSpec((1, CHUNK, BLK, BLK), x_block),
                 pl.BlockSpec((1, BLK, BLK), m_block),
                 pl.BlockSpec((512, R), whole),
                 pl.BlockSpec((1024, R), whole),
@@ -264,12 +352,10 @@
                 pl.BlockSpec((512, R), whole),
             ),
             scratch_shapes=[
-                pltpu.VMEM((CHUNK, BLK, BLK), F32),
                 pltpu.VMEM((BLK, R), F32),
                 pltpu.VMEM((BLK, R), F32),
                 pltpu.VMEM((CHUNK, 8, R), F32),
                 pltpu.VMEM((BLK, R), F32),
-                pltpu.VMEM((256, 256), BF16),
                 pltpu.VMEM((CHUNK * BLK, R), BF16),
                 pltpu.VMEM((BLK, CHUNK * BLK), BF16),
             ],
@@ -286,6 +372,7 @@
     me = Place()
     copies = Copies(send_sems, recv_sems)
     me.greet()
+    me.met()
     other = me.at(core=1 - me.core)
     left, right = slice(0, 128), slice(128, 256)
     in_b, in_d = [], []
@@ -411,9 +498,11 @@
 
 
 def per_device(tensor_blocks, fiber_mask, block_coords, block_counts, factor_a, factor_b, factor_c):
-    a, b, c = gather(factor_a, factor_b, factor_c)
+    a, b, c, turned = gather(
+        factor_a, factor_b, factor_c, tensor_blocks.reshape(SLOTS, BLK, BLK, BLK)
+    )
     ga, gb, gc = terms(
-        tensor_blocks.reshape(SLOTS, BLK, BLK, BLK),
+        turned,
         fiber_mask.reshape(SLOTS, BLK, BLK),
         block_coords.reshape(3, 1, SLOTS),
         block_counts.reshape(1),

time: 93.3 us -> 98.1 us (1.051)
  the two profiles are of different devices: /device:TPU:4 before, /device:TPU:1 now
where the time goes in v3:
time: 98.1 us; the launch traced here: 96.8 us
  Pallas kernels  95.5 us (97%)
  between operations  1.29 us (1%)
    pallas_call x1, Pallas kernels, terms(): pl.pallas_call(terms_kernel, out_shape=(jax.ShapeDtypeStruct((512, R), F3...  33.8 us
    pallas_call x1, Pallas kernels, gather(): pl.pallas_call(gather_kernel, out_shape=(jax.ShapeDtypeStruct((4, NZ, SHA...  33.7 us
    pallas_call x1, Pallas kernels, scatter(): pl.pallas_call(scatter_kernel, out_shape=jax.ShapeDtypeStruct((3, SHARD,...  26.6 us

profile of v3, /device:TPU:1, one launch (start us, length us, event | category | flops | bytes accessed | tf_op | source)
XLA Modules:
  0.0 96.8 jit_solution(9622077864767022428)
XLA Ops:
  1.3 33.7 %gather.1 = (bf16[4,8,16,256]{3,2,1,0:T(8,128)(2,1)}, bf16[8,8,16,256]{3,2,1,0:T(8,128)(2,1)}, bf16[4,8,16,256]{3,2,1,0:T(8,128)(2,1)}, bf16[24,16,128,128]{3,2,1,0:T(8,128)(2,1)}) custom-call(bf16[1,16,256]{2,1,0:T(8,128)(2,1)} %fa.1, bf16[1,16,256]{2,1,0:T(8,128)(2,1)} %fb.1, bf16[1,16,256]{2,1,0:T(8,128)(2,1)} %fc.1, bf16[3,128,128,128]{3,2,1,0:T(8,128)(2,1)} %bitcast.12), custom_call_target="tpu_custom_call" | custom-call | tf_op jit(solution)/shard_map/gather/pallas_call | solution.py:225
  35.0 33.8 %terms.1 = (f32[512,256]{1,0:T(8,128)}, f32[1024,256]{1,0:T(8,128)}, f32[512,256]{1,0:T(8,128)}) custom-call(s32[3,1,3]{2,1,0:T(1,128)} %bitcast.21, s32[1]{0:T(128)} %bitcast.11.filled, bf16[3,128,128,128]{3,2,1,0:T(8,128)(2,1)} %bitcast.13, s32[3,128,128]{2,1,0:T(8,128)} %bitcast.20, bf16[512,256]{1,0:T(8,128)(2,1)} %bitcast.18, ...), custom_call_target="tpu_custom_call" | custom-call | tf_op jit(solution)/shard_map/terms/pallas_call | solution.py:332
  68.8 26.6 %scatter.1.rows = f32[3,16,256]{2,1,0:T(8,128)} custom-call(f32[2,2,8,16,256]{4,3,2,1,0:T(8,128)} %bitcast.16, f32[4,2,8,16,256]{4,3,2,1,0:T(8,128)} %bitcast.14, f32[16,2,16,256]{3,2,1,0:T(8,128)} %bitcast.17), custom_call_target="tpu_custom_call" | custom-call | tf_op jit(solution)/shard_map/scatter/pallas_call | solution.py:462
  95.4 1.4 %part.1 = (f32[1,16,256]{2,1,0:T(8,128)}, f32[1,16,256]{2,1,0:T(8,128)}, f32[1,16,256]{2,1,0:T(8,128)}) custom-call(f32[3,16,256]{2,1,0:T(8,128)} %scatter.1.rows), custom_call_target="tpu_custom_call" | custom-call | tf_op jit(solution)/shard_map/part/pallas_call | solution.py:486

commit v4 on v3

--- a/solution.py
+++ b/solution.py
@@ -15,6 +15,8 @@
 CHUNK = 16
 CHUNKS = BLK // CHUNK
 NV = 8
+VMEM_LIMIT = 50 << 20
+DEPTH = 6
 UNIT = 8
 F32 = jnp.float32
 BF16 = jnp.bfloat16
@@ -85,37 +87,38 @@
         return x.at[i // CHUNKS, :, pl.ds(pl.multiple_of(i % CHUNKS * CHUNK, CHUNK), CHUNK), :]
 
     def load(i):
-        return pltpu.make_async_copy(source(i), xin.at[i % 2], in_sems.at[i % 2])
+        return pltpu.make_async_copy(source(i), xin.at[i % DEPTH], in_sems.at[i % DEPTH])
 
     def store(i):
-        return pltpu.make_async_copy(xout.at[i % 2], xt.at[i], out_sems.at[i % 2])
+        return pltpu.make_async_copy(xout.at[i % DEPTH], xt.at[i], out_sems.at[i % DEPTH])
 
     if lo == 0:
-        load(0).start()
+        for i in range(DEPTH - 1):
+            load(i).start()
 
     def body(i, carry):
         load(i).wait()
 
-        @pl.when(i < SLOTS * CHUNKS - 1)
+        @pl.when(i <= SLOTS * CHUNKS - DEPTH)
         def _():
-            load(i + 1).start()
-
-        @pl.when(i >= 2)
+            load(i + DEPTH - 1).start()
+
+        @pl.when(i >= DEPTH)
         def _():
-            store(i - 2).wait()
+            store(i - DEPTH).wait()
 
         for g in range(BLK // UNIT):
             us = slice(UNIT * g, UNIT * g + UNIT)
-            rows = xin[i % 2, us].reshape(UNIT * CHUNK, BLK)
+            rows = xin[i % DEPTH, us].reshape(UNIT * CHUNK, BLK)
             rows = jnp.dot(perm[...], rows, preferred_element_type=F32).astype(BF16)
-            xout[i % 2, :, us, :] = rows.reshape(CHUNK, UNIT, BLK)
+            xout[i % DEPTH, :, us, :] = rows.reshape(CHUNK, UNIT, BLK)
         store(i).start()
         return carry
 
     lax.fori_loop(lo, hi, body, 0)
     if hi == SLOTS * CHUNKS:
-        store(hi - 2).wait()
-        store(hi - 1).wait()
+        for i in range(hi - DEPTH, hi):
+            store(i).wait()
 
 
 NEAR = (0, 7, 1, 6, 2, 5, 3, 4)
@@ -132,7 +135,6 @@
     block_a = me.x_hi * 2 + me.core
     block_b = me.y * 2 + me.x_lo
     block_c = (me.x_lo * 2 + me.x_hi) * 2 + me.core
-    me.greet()
     own = [
         pltpu.make_async_copy(fb.at[0], b.at[block_b, me.z], own_sems.at[0]),
         pltpu.make_async_copy(fa.at[0], a.at[block_a, me.z], own_sems.at[1]),
@@ -140,19 +142,22 @@
     ]
     for copy in own:
         copy.start()
+    me.greet()
     row = lax.broadcasted_iota(jnp.int32, perm.shape, 0)
     col = lax.broadcasted_iota(jnp.int32, perm.shape, 1)
     swapped = (row % UNIT) * CHUNK + row // UNIT
     perm[...] = jnp.where(col == swapped, 1.0, 0.0).astype(BF16)
     turn(0, 4)
+    for copy in own:
+        copy.wait()
     me.met()
     z_b, z_a, y_c = {}, {}, []
     for k in reversed(NEAR[1:]):
-        z_b[k] = copies.start(fb.at[0], b.at[block_b, me.z], me.at(z=(me.z + k) % NZ))
+        z_b[k] = copies.start(b.at[block_b, me.z], b.at[block_b, me.z], me.at(z=(me.z + k) % NZ))
     for k in range(1, NY):
-        y_c.append(copies.start(fc.at[0], c.at[me.y, block_c], me.at(y=(me.y + k) % NY)))
+        y_c.append(copies.start(c.at[me.y, block_c], c.at[me.y, block_c], me.at(y=(me.y + k) % NY)))
     for k in reversed(NEAR[1:]):
-        z_a[k] = copies.start(fa.at[0], a.at[block_a, me.z], me.at(z=(me.z + k) % NZ))
+        z_a[k] = copies.start(a.at[block_a, me.z], a.at[block_a, me.z], me.at(z=(me.z + k) % NZ))
     up, down = me.at(y=(me.y + 1) % NY), me.at(y=(me.y + NY - 1) % NY)
     above, below = (me.y + 1) % NY, (me.y + NY - 1) % NY
     beside = me.at(x_lo=1 - me.x_lo)
@@ -163,8 +168,6 @@
     def send(ref, peer):
         return copies.start(ref, ref, peer)
 
-    for copy in own:
-        copy.wait()
     to_x, to_up, to_down = {}, {}, {}
 
     def spread(k):
@@ -230,21 +233,23 @@
             jax.ShapeDtypeStruct((4, 8, SHARD, R), BF16),
             jax.ShapeDtypeStruct((SLOTS * CHUNKS, CHUNK, BLK, BLK), BF16),
         ),
-        in_specs=[VMEM] * 3 + [pl.BlockSpec(memory_space=pl.ANY)],
+        in_specs=[pl.BlockSpec(memory_space=pl.ANY)] * 4,
         out_specs=(VMEM,) * 3 + (pl.BlockSpec(memory_space=pl.ANY),),
         scratch_shapes=[
-            pltpu.VMEM((2, BLK, CHUNK, BLK), BF16),
-            pltpu.VMEM((2, CHUNK, BLK, BLK), BF16),
+            pltpu.VMEM((DEPTH, BLK, CHUNK, BLK), BF16),
+            pltpu.VMEM((DEPTH, CHUNK, BLK, BLK), BF16),
             pltpu.VMEM((UNIT * CHUNK, UNIT * CHUNK), BF16),
             pltpu.SemaphoreType.DMA((n,)),
             pltpu.SemaphoreType.DMA((n,)),
             pltpu.SemaphoreType.DMA((3,)),
-            pltpu.SemaphoreType.DMA((2,)),
-            pltpu.SemaphoreType.DMA((2,)),
+            pltpu.SemaphoreType.DMA((DEPTH,)),
+            pltpu.SemaphoreType.DMA((DEPTH,)),
         ],
-        compiler_params=pltpu.CompilerParams(collective_id=0, has_side_effects=True),
+        compiler_params=pltpu.CompilerParams(
+            collective_id=0, has_side_effects=True, vmem_limit_bytes=VMEM_LIMIT
+        ),
         name="gather",
-    )(fa, fb, fc, x)
+    )(*(pltpu.with_memory_space_constraint(arg, pltpu.HBM) for arg in (fa, fb, fc, x)))
     return (
         a.reshape(512, R), b.reshape(1024, R), c.reshape(512, R), xt.reshape(SLOTS, BLK, BLK, BLK)
     )
@@ -261,7 +266,7 @@
         gb[...] = jnp.zeros_like(gb)
         gc[...] = jnp.zeros_like(gc)
 
-    @pl.when(slot < filled[0])
+    @pl.when(slot < filled[0, 0, 0])
     def _():
         start_a = pl.multiple_of(coords[0, 0, slot] * BLK, BLK)
         start_b = pl.multiple_of(coords[1, 0, slot] * BLK, BLK)
@@ -317,16 +322,13 @@
 
 
 def terms(blocks, fibers, coords, filled, a, b, c):
-    def held(slot, filled):
-        return jnp.minimum(slot, jnp.maximum(filled[0] - 1, 0))
-
-    def x_block(slot, chunk, coords, filled):
-        return (held(slot, filled), jnp.where(slot < filled[0], chunk, CHUNKS - 1), 0, 0)
-
-    def m_block(slot, chunk, coords, filled):
-        return (held(slot, filled), 0, 0)
-
-    def whole(slot, chunk, coords, filled):
+    def x_block(slot, chunk, coords):
+        return (slot, chunk, 0, 0)
+
+    def m_block(slot, chunk, coords):
+        return (slot, 0, 0)
+
+    def whole(slot, chunk, coords):
         return (0, 0)
 
     return pl.pallas_call(
@@ -337,9 +339,10 @@
             jax.ShapeDtypeStruct((512, R), F32),
         ),
         grid_spec=pltpu.PrefetchScalarGridSpec(
-            num_scalar_prefetch=2,
+            num_scalar_prefetch=1,
             grid=(SLOTS, CHUNKS),
             in_specs=[
+                pl.BlockSpec(memory_space=pltpu.SMEM),
                 pl.BlockSpec((1, CHUNK, BLK, BLK), x_block),
                 pl.BlockSpec((1, BLK, BLK), m_block),
                 pl.BlockSpec((512, R), whole),
@@ -360,6 +363,7 @@
                 pltpu.VMEM((BLK, CHUNK * BLK), BF16),
             ],
         ),
+        compiler_params=pltpu.CompilerParams(vmem_limit_bytes=VMEM_LIMIT),
         name="terms",
     )(coords, filled, blocks, fibers, a, b, c)
 
@@ -476,7 +480,9 @@
             pltpu.SemaphoreType.DMA((n,)),
             pltpu.SemaphoreType.DMA((n,)),
         ],
-        compiler_params=pltpu.CompilerParams(collective_id=1, has_side_effects=True),
+        compiler_params=pltpu.CompilerParams(
+            collective_id=1, has_side_effects=True, vmem_limit_bytes=VMEM_LIMIT
+        ),
         name="scatter",
     )(
         ga.reshape(2, 2, NZ, SHARD, R),
@@ -488,6 +494,7 @@
         out_shape=(jax.ShapeDtypeStruct((1, SHARD, R), F32),) * 3,
         in_specs=[VMEM],
         out_specs=(VMEM,) * 3,
+        compiler_params=pltpu.CompilerParams(vmem_limit_bytes=VMEM_LIMIT),
         name="part",
     )(out)
 
@@ -505,7 +512,7 @@
         turned,
         fiber_mask.reshape(SLOTS, BLK, BLK),
         block_coords.reshape(3, 1, SLOTS),
-        block_counts.reshape(1),
+        block_counts,
         a, b, c,
     )
     return scatter(ga, gb, gc)

time: 98.1 us -> 80 us (0.82)
  the two profiles are of different devices: /device:TPU:1 before, /device:TPU:4 now
where the time goes in v4:
time: 80 us; the launch traced here: 79.6 us
  Pallas kernels  78.2 us (98%)
  between operations  1.37 us (2%)
    pallas_call x1, Pallas kernels, scatter(): pl.pallas_call(scatter_kernel, out_shape=jax.ShapeDtypeStruct((3, SHARD,...  33.4 us
    pallas_call x1, Pallas kernels, gather(): pl.pallas_call(gather_kernel, out_shape=(jax.ShapeDtypeStruct((4, NZ, SHA...  24 us
    pallas_call x1, Pallas kernels, terms(): pl.pallas_call(terms_kernel, out_shape=(jax.ShapeDtypeStruct((512, R), F3...  20.2 us

profile of v4, /device:TPU:4, one launch (start us, length us, event | category | flops | bytes accessed | tf_op | source)
XLA Modules:
  0.0 79.6 jit_solution(8523638781676706319)
XLA Ops:
  0.6 0.0 copy-start.1
  0.6 0.0 copy-start
  1.3 24.0 %gather.1 = (bf16[4,8,16,256]{3,2,1,0:T(8,128)(2,1)S(1)}, bf16[8,8,16,256]{3,2,1,0:T(8,128)(2,1)S(1)}, bf16[4,8,16,256]{3,2,1,0:T(8,128)(2,1)S(1)}, bf16[24,16,128,128]{3,2,1,0:T(8,128)(2,1)}) custom-call(bf16[1,16,256]{2,1,0:T(8,128)(2,1)} %fa.1, bf16[1,16,256]{2,1,0:T(8,128)(2,1)} %fb.1, bf16[1,16,256]{2,1,0:T(8,128)(2,1)} %fc.1, ...), custom_call_target="tpu_custom_call" | custom-call | tf_op jit(solution)/shard_map/gather/pallas_call | solution.py:228
  25.4 0.0 copy-done.1
  25.4 0.0 copy-done
  25.4 20.2 %terms.1 = (f32[512,256]{1,0:T(8,128)S(1)}, f32[1024,256]{1,0:T(8,128)S(1)}, f32[512,256]{1,0:T(8,128)S(1)}) custom-call(s32[3,1,3]{2,1,0:T(1,128)S(1)} %bitcast.17, s32[1,1,1]{2,1,0:T(1,128)S(6)} %copy.10.filled, bf16[3,128,128,128]{3,2,1,0:T(8,128)(2,1)} %bitcast.19, s32[3,128,128]{2,1,0:T(8,128)S(1)} %bitcast.16, bf16[512,256]{1,0:T(8,128)(2,1)S(1)} %bitcast.14, ...), custom_call_target="tpu_custom_call" | custom-call | tf_op jit(solution)/shard_map/terms/pallas_call | solution.py:334
  45.6 33.4 %scatter.1.rows = f32[3,16,256]{2,1,0:T(8,128)S(1)} custom-call(f32[2,2,8,16,256]{4,3,2,1,0:T(8,128)S(1)} %bitcast.12, f32[4,2,8,16,256]{4,3,2,1,0:T(8,128)S(1)} %bitcast.10, f32[16,2,16,256]{3,2,1,0:T(8,128)S(1)} %bitcast.13), custom_call_target="tpu_custom_call" | custom-call | tf_op jit(solution)/shard_map/scatter/pallas_call | solution.py:466
  78.9 0.6 part.1
Async XLA Ops:
  0.6 24.8 %copy-start.1 = (s32[1,1,1,3,3]{4,2,3,1,0:T(1,128)S(1)}, s32[1,1,1,3,3]{4,2,3,1,0:T(1,128)}, u32[]{:S(2)}) copy-start(s32[1,1,1,3,3]{4,2,3,1,0:T(1,128)} %param.9) | copy-start | bytes 112
  0.6 24.8 %copy-start = (s32[1,1,1,3,128,128]{5,4,3,2,1,0:T(8,128)S(1)}, s32[1,1,1,3,128,128]{5,4,3,2,1,0:T(8,128)}, u32[]{:S(2)}) copy-start(s32[1,1,1,3,128,128]{5,4,3,2,1,0:T(8,128)} %param.8) | copy-start | bytes 589828
